TPU v7x, 256 devices: a whole 4x4x8 slice. The times are simulated.
256 devices in a mesh: branch: 2 (over core), gi: 16 (over y_hi, z), gj: 8 (over x, y_lo).
Axes of the slice: x: 4, y: 4 (y_hi: 2, y_lo: 2; y = y_hi * 2 + y_lo), z: 8, core: 2. Of those that a mesh axis runs over, the one named last changes fastest.
Arguments:
- homolog_embedding: float32 [128, 256, 256], P(('branch', 'gj'), 'gi'), may hold values from -6 to 6
- pair_input_tensor: float32 [256, 256, 128], P('gi', ('branch', 'gj')), may hold values from -6 to 6
- layernorm_scales: float32 [4, 256], replicated, may hold values from 0.5 to 1.5
- pair_norm_gains: float32 [3, 128], replicated, may hold values from 0.5 to 1.5
- pair_bias_matrix: float32 [128, 8], replicated
- horizontal_qkvg_kernel: float32 [256, 1024], replicated, may hold values from -0.375 to 0.375
- horizontal_final_kernel: float32 [256, 256], replicated, may hold values from -0.375 to 0.375
- vertical_qkvg_kernel: float32 [256, 1024], replicated, may hold values from -0.375 to 0.375
- vertical_final_kernel: float32 [256, 256], replicated, may hold values from -0.375 to 0.375
- feedforward_expand_kernel: float32 [256, 1024], replicated, may hold values from -0.375 to 0.375
- feedforward_shrink_kernel: float32 [1024, 256], replicated, may hold values from -0.1875 to 0.1875
- dyadic_sides_kernel: float32 [256, 64], replicated, may hold values from -0.375 to 0.375
- outer_output_matrix: float32 [1024, 128], replicated, may hold values from -1 to 1
- triangle_input_matrix: float32 [128, 640], replicated, may hold values from -0.5 to 0.5
- triangle_output_matrix: float32 [128, 128], replicated, may hold values from -0.5 to 0.5
Outputs:
- alignment_output: float32 [128, 256, 256], P(('branch', 'gj'), 'gi')
- pair_output_tensor: float32 [256, 256, 128], P('gi', ('branch', 'gj'))
All inputs are finite; a program needn't handle non-finite values.
Results may differ from a plain program's by a relative error of at most 0.0003.
Values sent between devices are 32-bit elements; how exact they have to be, the bound alone decides.
A program may use at most 64 MiB of HBM per device.

v0:
```python
import math
import jax
import jax.numpy as jnp
from jax import lax
from jax.sharding import PartitionSpec as P

epsilon = 1e-05
highest = lax.Precision.HIGHEST
lowest_start = -1e30


def from_root(shard, axis, root):
    mine = lax.axis_index(axis) == root
    return lax.psum(jnp.where(mine, shard, jnp.zeros_like(shard)), axis)


def layer_normalise(values, norm_gain):
    average = jnp.mean(values, axis=-1, keepdims=True)
    centred = values - average
    variance = jnp.mean(centred * centred, axis=-1, keepdims=True)
    return centred * lax.rsqrt(variance + epsilon) * norm_gain


def apply_projection(values, weight):
    return jnp.einsum("...c,cd->...d", values, weight, precision=highest)


def transition_update(values, norm_gain, feedforward_expand_kernel, feedforward_shrink_kernel):
    expanded = jax.nn.relu(
        apply_projection(layer_normalise(values, norm_gain), feedforward_expand_kernel)
    )
    return values + apply_projection(expanded, feedforward_shrink_kernel)


def online_update(state_carry, scores, values, einsum_form):
    running_max, sum_weights, numerator = state_carry
    new_max = jnp.maximum(running_max, jnp.max(scores, axis=-1))
    weights = jnp.exp(scores - new_max[..., None])
    sum_weights = jnp.sum(weights, axis=-1)
    numerator = jnp.einsum(einsum_form, weights, values, precision=highest)
    return (new_max, sum_weights, numerator)


def empty_state(leading, head_size):
    return (
        jnp.full(leading, lowest_start, jnp.float32),
        jnp.zeros(leading, jnp.float32),
        jnp.zeros(leading + (head_size,), jnp.float32),
    )


def panels(first_local, second_local):
    groups = lax.axis_size("gi") // lax.axis_size(("branch", "gj"))
    col_index = lax.axis_index(("branch", "gj"))
    first_panel, second_panel = (
        lax.all_gather(first_local, ("branch", "gj"), axis=1, tiled=True),
        lax.all_gather(second_local, ("branch", "gj"), axis=1, tiled=True),
    )
    pieces = from_root(second_panel, "gi", col_index * groups + 0)
    return (first_panel, pieces)


def per_device(
    homolog_embedding,
    pair_input_tensor,
    layernorm_scales,
    pair_norm_gains,
    pair_bias_matrix,
    horizontal_qkvg_kernel,
    horizontal_final_kernel,
    vertical_qkvg_kernel,
    vertical_final_kernel,
    feedforward_expand_kernel,
    feedforward_shrink_kernel,
    dyadic_sides_kernel,
    outer_output_matrix,
    triangle_input_matrix,
    triangle_output_matrix,
):
    rows_per_device, residues_per_device, alignment_width = homolog_embedding.shape
    pair_cols, pair_width = (pair_input_tensor.shape[1], pair_input_tensor.shape[2])
    head_count = pair_bias_matrix.shape[1]
    inner_feature_width = horizontal_final_kernel.shape[0]
    head_size = inner_feature_width // head_count
    outer_width = dyadic_sides_kernel.shape[1] // 2
    bias_local = apply_projection(
        layer_normalise(pair_input_tensor, pair_norm_gains[0]), pair_bias_matrix
    ).reshape(residues_per_device, pair_cols * head_count)
    bias_rows = lax.all_gather(bias_local, ("branch", "gj"), axis=1, tiled=True).reshape(
        residues_per_device, -1, head_count
    )
    bias_heads = jnp.transpose(bias_rows, (2, 0, 1))
    alignment_normalised = layer_normalise(homolog_embedding, layernorm_scales[0])
    row_query_values = apply_projection(
        alignment_normalised, horizontal_qkvg_kernel[:, :inner_feature_width]
    ).reshape(rows_per_device, residues_per_device, head_count, head_size)
    row_gate_values = apply_projection(
        alignment_normalised, horizontal_qkvg_kernel[:, 3 * inner_feature_width :]
    )
    row_start = empty_state((rows_per_device, head_count, residues_per_device), head_size)
    row_pair_slice = apply_projection(
        alignment_normalised,
        horizontal_qkvg_kernel[:, inner_feature_width : 3 * inner_feature_width],
    )
    pieces = (
        lax.all_gather(row_pair_slice[..., :inner_feature_width], "gi", axis=1, tiled=True),
        lax.all_gather(row_pair_slice[..., inner_feature_width:], "gi", axis=1, tiled=True),
    )
    key_flat = pieces[0]
    block_rows = key_flat.shape[1]
    key_block = key_flat.reshape(rows_per_device, block_rows, head_count, head_size)
    value_block = pieces[1].reshape(rows_per_device, block_rows, head_count, head_size)
    scores = (
        jnp.einsum("sihd,sjhd->shij", row_query_values, key_block, precision=highest)
        / math.sqrt(head_size)
        + bias_heads[None]
    )
    row_state = online_update(row_start, scores, value_block, "shij,sjhd->shid")
    row_heads = row_state[2] / row_state[1][..., None]
    row_attention_result = jnp.transpose(row_heads, (0, 2, 1, 3)).reshape(
        rows_per_device, residues_per_device, inner_feature_width
    )
    alignment_after_rows = homolog_embedding + apply_projection(
        jax.nn.sigmoid(row_gate_values) * row_attention_result, horizontal_final_kernel
    )
    column_normalised = layer_normalise(alignment_after_rows, layernorm_scales[1])
    column_query = apply_projection(
        column_normalised, vertical_qkvg_kernel[:, :inner_feature_width]
    ).reshape(rows_per_device, residues_per_device, head_count, head_size)
    column_pairs = apply_projection(
        column_normalised, vertical_qkvg_kernel[:, inner_feature_width : 3 * inner_feature_width]
    )
    column_gate_values = apply_projection(
        column_normalised, vertical_qkvg_kernel[:, 3 * inner_feature_width :]
    )
    column_start = empty_state((residues_per_device, head_count, rows_per_device), head_size)
    pieces = (
        lax.all_gather(
            column_pairs[..., :inner_feature_width], ("branch", "gj"), axis=0, tiled=True
        ),
        lax.all_gather(
            column_pairs[..., inner_feature_width:], ("branch", "gj"), axis=0, tiled=True
        ),
    )
    block_rows = pieces[0].shape[0]
    key_block = pieces[0].reshape(block_rows, residues_per_device, head_count, head_size)
    value_block = pieces[1].reshape(block_rows, residues_per_device, head_count, head_size)
    scores = jnp.einsum("sihd,tihd->ihst", column_query, key_block, precision=highest) / math.sqrt(
        head_size
    )
    column_state = online_update(column_start, scores, value_block, "ihst,tihd->ihsd")
    column_heads = column_state[2] / column_state[1][..., None]
    column_attention_result = jnp.transpose(column_heads, (2, 0, 1, 3)).reshape(
        rows_per_device, residues_per_device, inner_feature_width
    )
    alignment_after_columns = alignment_after_rows + apply_projection(
        jax.nn.sigmoid(column_gate_values) * column_attention_result, vertical_final_kernel
    )
    alignment_output = transition_update(
        alignment_after_columns,
        layernorm_scales[2],
        feedforward_expand_kernel,
        feedforward_shrink_kernel,
    )
    factor_pair = apply_projection(
        layer_normalise(alignment_output, layernorm_scales[3]), dyadic_sides_kernel
    )
    left_local = jnp.transpose(factor_pair[..., :outer_width], (1, 0, 2)).reshape(
        residues_per_device, rows_per_device * outer_width
    )
    right_local = jnp.transpose(factor_pair[..., outer_width:], (1, 0, 2)).reshape(
        residues_per_device, rows_per_device * outer_width
    )
    left_panel, right_panel = panels(left_local, right_local)
    all_rows = left_panel.shape[1] // outer_width
    left_three = left_panel.reshape(residues_per_device, all_rows, outer_width)
    right_three = right_panel.reshape(pair_cols, all_rows, outer_width)
    outer = jnp.einsum("isc,jsd->ijcd", left_three, right_three, precision=highest) / all_rows
    pair_first = pair_input_tensor + apply_projection(
        outer.reshape(residues_per_device, pair_cols, outer_width * outer_width),
        outer_output_matrix,
    )
    projected_values = apply_projection(
        layer_normalise(pair_first, pair_norm_gains[1]), triangle_input_matrix
    )
    left_tri = (
        jax.nn.sigmoid(projected_values[..., pair_width : 2 * pair_width])
        * projected_values[..., :pair_width]
    )
    right_tri = (
        jax.nn.sigmoid(projected_values[..., 3 * pair_width : 4 * pair_width])
        * projected_values[..., 2 * pair_width : 3 * pair_width]
    )
    out_gate = projected_values[..., 4 * pair_width :]
    left_rows, right_rows = panels(
        left_tri.reshape(residues_per_device, pair_cols * pair_width),
        right_tri.reshape(residues_per_device, pair_cols * pair_width),
    )
    left_rows = left_rows.reshape(residues_per_device, -1, pair_width)
    right_rows = right_rows.reshape(pair_cols, -1, pair_width)
    product = jnp.einsum("ikc,jkc->ijc", left_rows, right_rows, precision=highest)
    pair_output_tensor = pair_first + jax.nn.sigmoid(out_gate) * apply_projection(
        layer_normalise(product, pair_norm_gains[2]), triangle_output_matrix
    )
    return (alignment_output, pair_output_tensor)


def solution(mesh):
    return jax.shard_map(
        per_device,
        mesh=mesh,
        in_specs=(
            P(("branch", "gj"), "gi", None),
            P("gi", ("branch", "gj"), None),
            P(),
            P(),
            P(),
            P(),
            P(),
            P(),
            P(),
            P(),
            P(),
            P(),
            P(),
            P(),
            P(),
        ),
        out_specs=(P(("branch", "gj"), "gi", None), P("gi", ("branch", "gj"), None)),
        check_vma=False,
    )
```

profile of v0, /device:TPU:2, one launch (start us, length us, event | category | flops | bytes accessed | tf_op | source)
XLA Modules:
  0.0 740.1 jit_solution(3773819482061920002)
XLA Ops:
  9.5 1.4 fusion.100
  10.8 1.6 fusion.19
  17.5 40.2 %all_gather.28 = f32[16,2048]{0,1:T(8,128)S(1)} all-gather(f32[16,128]{0,1:T(8,128)S(1)} %convolution_bitcast_fusion.2), channel_id=1, replica_groups=mesh['branch'=2,'gi'=16,'gj'=8] {'branch','gj'}, dimensions={1}, use_global_device_ids=true | all-gather | bytes 139264 | tf_op jit(solution)/shard_map/all_gather | solution.py:89
  58.1 44.4 %all-gather.7.cloned.1.call-done = f32[8,256,256]{2,1,0:T(8,128)} async-done(((f32[8,16,256]{2,1,0:T(8,128)}), f32[8,256,256]{2,1,0:T(8,128)}) %all-gather.7.cloned.1.call-update) | async-done | bytes 2097168 | tf_op jit(solution)/shard_map/all_gather | solution.py:106
  102.4 2.9 copy.90
  105.4 2.9 fusion.101
  108.7 79.0 %all-gather.9.cloned.1.call-done = f32[8,256,256]{2,1,0:T(8,128)} async-done(((f32[8,16,256]{2,1,0:T(8,128)}), f32[8,256,256]{2,1,0:T(8,128)}) %all-gather.9.cloned.1.call-update) | async-done | bytes 2097168 | tf_op jit(solution)/shard_map/all_gather | solution.py:107
  187.7 2.9 copy.94
  190.6 3.5 fusion.1
  195.9 1.3 fusion.102
  200.7 30.8 %all-gather.11.cloned.1.call-done = f32[128,16,256]{2,1,0:T(8,128)} async-done(((f32[8,16,256]{2,1,0:T(8,128)}), f32[128,16,256]{2,1,0:T(8,128)}) %all-gather.11.cloned.1.call-update) | async-done | bytes 2097168 | tf_op jit(solution)/shard_map/all_gather | solution.py:138
  231.4 2.0 copy.96
  233.4 3.2 fusion.103
  237.8 32.4 %all-gather.13.cloned.1.call-done = f32[128,16,256]{2,1,0:T(8,128)} async-done(((f32[8,16,256]{2,1,0:T(8,128)}), f32[128,16,256]{2,1,0:T(8,128)}) %all-gather.13.cloned.1.call-update) | async-done | bytes 2097168 | tf_op jit(solution)/shard_map/all_gather | solution.py:141
  270.2 2.0 copy.98
  272.2 4.5 fusion.2
  277.0 1.6 fusion.6
  281.4 28.4 %all_gather.32 = f32[16,4096]{1,0:T(8,128)S(1)} all-gather(f32[16,256]{1,0:T(8,128)S(1)} %reshape.171), channel_id=1, replica_groups=mesh['branch'=2,'gi'=16,'gj'=8] {'branch','gj'}, dimensions={1}, use_global_device_ids=true | all-gather | bytes 278528 | tf_op jit(solution)/shard_map/all_gather | solution.py:57
  311.3 28.2 %all_gather.33 = f32[16,4096]{1,0:T(8,128)S(1)} all-gather(f32[16,256]{1,0:T(8,128)S(1)} %reshape.173), channel_id=1, replica_groups=mesh['branch'=2,'gi'=16,'gj'=8] {'branch','gj'}, dimensions={1}, use_global_device_ids=true | all-gather | bytes 278528 | tf_op jit(solution)/shard_map/all_gather | solution.py:56
  339.8 128.2 %all-reduce.3.cloned.1.call-done = f32[16,128,32]{1,2,0:T(8,128)} async-done(((f32[16,128,32]{1,2,0:T(8,128)}), f32[16,128,32]{1,2,0:T(8,128)}) %all-reduce.3.cloned.1.call-update) | async-done | bytes 262160 | tf_op jit(solution)/shard_map/psum | solution.py:14
  468.1 5.9 multiply_bitcast_fusion
  473.9 5.4 copy.104
  479.3 3.8 reshape.175
  487.7 32.8 %all-gather.15.cloned.1.call-done = f32[16,32768]{1,0:T(8,128)} async-done(((f32[16,2048]{1,0:T(8,128)}), f32[16,32768]{1,0:T(8,128)}) %all-gather.15.cloned.1.call-update) | async-done | bytes 2097168 | tf_op jit(solution)/shard_map/all_gather | solution.py:57
  521.0 2.1 copy.105
  523.1 35.6 %all-gather.17.cloned.1.call-done = f32[16,32768]{1,0:T(8,128)} async-done(((f32[16,2048]{1,0:T(8,128)}), f32[16,32768]{1,0:T(8,128)}) %all-gather.17.cloned.1.call-update) | async-done | bytes 2097168 | tf_op jit(solution)/shard_map/all_gather | solution.py:56
  558.7 3.3 copy.122
  562.1 2.2 copy.106
  564.4 160.5 %all-reduce.5.cloned.1.call-done = f32[16,256,128]{1,0,2:T(8,128)} async-done(((f32[16,256,128]{1,0,2:T(8,128)}), f32[16,256,128]{1,0,2:T(8,128)}) %all-reduce.5.cloned.1.call-update) | async-done | bytes 2097168 | tf_op jit(solution)/shard_map/psum | solution.py:14
  724.8 4.6 bitcast_reduce_fusion
  729.5 1.6 copy.107
  731.4 1.9 fusion.11
  (116 shorter events, 24.4 us)
Async XLA Ops:
  7.2 272.0 %copy-start = (f32[256,1024]{1,0:T(8,128)S(1)}, f32[256,1024]{1,0:T(8,128)}, u32[]{:S(2)}) copy-start(f32[256,1024]{1,0:T(8,128)} %param.24) | copy-start | bytes 3145732
  7.2 6.9 copy-start.2
  7.2 6.7 copy-start.4
  7.2 8.5 %copy-start.15 = (f32[3,128]{1,0:T(4,128)S(1)}, f32[3,128]{1,0:T(4,128)}, u32[]{:S(2)}) copy-start(f32[3,128]{1,0:T(4,128)} %param.18) | copy-start | bytes 4612
  7.2 9.3 %copy-start.13 = (f32[128,8]{0,1:T(8,128)S(1)}, f32[128,8]{0,1:T(8,128)}, u32[]{:S(2)}) copy-start(f32[128,8]{0,1:T(8,128)} %param.19) | copy-start | bytes 12292
  7.2 95.2 %all-gather.7.cloned.1.call-start = ((), (), s32[]{:S(2)}) async-start(), calls=%async_computation | async-start | bytes 2228224 | tf_op jit(solution)/shard_map/all_gather | solution.py:106
  13.1 174.6 %all-gather.9.cloned.1.call-start = ((), (), s32[]{:S(2)}) async-start(), calls=%async_computation.1 | async-start | bytes 2228224 | tf_op jit(solution)/shard_map/all_gather | solution.py:107
  13.9 217.6 %all-gather.11.cloned.1.call-start = ((), (), s32[]{:S(2)}) async-start(), calls=%async_computation.2 | async-start | bytes 2228224 | tf_op jit(solution)/shard_map/all_gather | solution.py:138
  194.2 3.2 copy-start.7
  198.6 71.6 %all-gather.13.cloned.1.call-start = ((), (), s32[]{:S(2)}) async-start(), calls=%async_computation.3 | async-start | bytes 2228224 | tf_op jit(solution)/shard_map/all_gather | solution.py:141
  199.2 268.9 %all-reduce.3.cloned.1.call-start = ((), (), s32[]{:S(2)}) async-start(), calls=%async_computation.4 | async-start | bytes 524288 | tf_op jit(solution)/shard_map/psum | solution.py:14
  236.6 0.8 copy-start.1
  276.6 1.9 copy-start.10
  276.6 2.5 copy-start.12
  276.8 3.1 copy-start.6
  278.9 1.9 copy-start.11
  280.6 30.5 %copy-start.5 = (f32[8,16,256]{2,1,0:T(8,128)}, f32[8,16,256]{2,1,0:T(8,128)S(1)}, u32[]{:S(2)}) copy-start(f32[8,16,256]{2,1,0:T(8,128)S(1)} %get-tuple-element.26) | copy-start | bytes 393220
  311.1 209.3 %all-gather.15.cloned.1.call-start = ((), (), s32[]{:S(2)}) async-start(), calls=%async_computation.5 | async-start | bytes 2228224 | tf_op jit(solution)/shard_map/all_gather | solution.py:57
  479.3 3.8 copy-start.8
  479.3 5.1 copy-start.14
  483.1 1.3 copy-start.9
  485.2 0.9 copy-start.3
  486.9 71.9 %all-gather.17.cloned.1.call-start = ((), (), s32[]{:S(2)}) async-start(), calls=%async_computation.7 | async-start | bytes 2228224 | tf_op jit(solution)/shard_map/all_gather | solution.py:56
  487.6 237.2 %all-reduce.5.cloned.1.call-start = ((), (), s32[]{:S(2)}) async-start(), calls=%async_computation.6 | async-start | bytes 4194304 | tf_op jit(solution)/shard_map/psum | solution.py:14
  564.3 167.1 %copy-start.16 = (f32[128]{0:T(128)S(1)}, f32[128]{0:T(128)}, u32[]{:S(2)}) copy-start(f32[128]{0:T(128)} %get-tuple-element.14) | copy-start | bytes 1540
  564.3 167.1 %copy-start.17 = (f32[128,128]{1,0:T(8,128)S(1)}, f32[128,128]{1,0:T(8,128)}, u32[]{:S(2)}) copy-start(f32[128,128]{1,0:T(8,128)} %param.29) | copy-start | bytes 196612
Sparse Core Ops, SparseCore 0:
  13.3 89.1 all-gather.6
  105.6 82.0 all-gather.8
  198.7 32.7 all-gather.10
  233.7 36.3 all-gather.12
  311.2 156.7 all-reduce.2
  487.0 33.4 all-gather.14
  522.3 36.3 all-gather.16
  561.4 163.4 all-reduce.4
where the time goes:
time: 741 us; the launch traced here: 740 us
  waiting for transfers between devices  545 us (74%)
  blocking collectives  96.8 us (13%)
  local copies, waits for them, and re-layouts  39.3 us (5%)
  matrix products  39.2 us (5%)
  between operations  14.8 us (2%)
    psum x2, waiting for transfers between devices, from_root(): return lax.psum(jnp.where(mine, shard, jnp.zeros_like(shard)), axis)  289 us
    all_gather x1, waiting for transfers between devices, per_device(): lax.all_gather(row_pair_slice[..., inner_feature_width:], 'gi', axis=1, t...  79 us
    all_gather x1, waiting for transfers between devices, per_device(): lax.all_gather(row_pair_slice[..., :inner_feature_width], 'gi', axis=1, t...  44.4 us
    all_gather x1, blocking collectives, per_device(): lax.all_gather(bias_local, ('branch', 'gj'), axis=1, tiled=True)  40.2 us
    all_gather x1, waiting for transfers between devices, panels(): lax.all_gather(first_local, ('branch', 'gj'), axis=1, tiled=True)  35.6 us
    all_gather x1, waiting for transfers between devices, panels(): lax.all_gather(second_local, ('branch', 'gj'), axis=1, tiled=True)  32.8 us
    all_gather x1, waiting for transfers between devices, per_device(): lax.all_gather(column_pairs[..., inner_feature_width:], ('branch', 'gj'),...  32.4 us
    all_gather x1, waiting for transfers between devices, per_device(): lax.all_gather(column_pairs[..., :inner_feature_width], ('branch', 'gj'),...  30.8 us
  transfers between devices with their start and end apart: 8, of which 8 were waited for; matrix products, arithmetic and copies ran while one was open for 4% of the time, Pallas kernels for 0%

commit v1 on v0

--- a/solution.py
+++ b/solution.py
@@ -52,8 +52,20 @@
 def panels(first_local, second_local):
     groups = lax.axis_size("gi") // lax.axis_size(("branch", "gj"))
     col_index = lax.axis_index(("branch", "gj"))
+
+    def update_keys_all(local):
+        return jnp.concatenate(
+            lax.all_to_all(
+                jnp.stack([local for _ in range(lax.axis_size(("branch", "gj")))]),
+                ("branch", "gj"),
+                0,
+                0,
+            ),
+            1,
+        )
+
     first_panel, second_panel = (
-        lax.all_gather(first_local, ("branch", "gj"), axis=1, tiled=True),
+        update_keys_all(first_local),
         lax.all_gather(second_local, ("branch", "gj"), axis=1, tiled=True),
     )
     pieces = from_root(second_panel, "gi", col_index * groups + 0)

time: 741 us -> 707 us (0.954)
  waiting for transfers between devices: 545 us -> 494 us
  blocking collectives: 96.8 us -> 116 us
    all_to_all x0 -> x2, blocking collectives: none -> 47 us  [update_keys_all(): lax.all_to_all(jnp.stack([local for _ in range(lax.axis_size(('branch', '...]
    all_gather x1 -> x0, waiting for transfers between devices: 35.6 us -> none  [panels(): lax.all_gather(first_local, ('branch', 'gj'), axis=1, tiled=True)]
    all_gather x1 -> x0, blocking collectives: 28.2 us -> none  [panels(): lax.all_gather(first_local, ('branch', 'gj'), axis=1, tiled=True)]
    psum x2, waiting for transfers between devices: 289 us -> 273 us  [from_root(): return lax.psum(jnp.where(mine, shard, jnp.zeros_like(shard)), axis)]
  transfers between devices with their start and end apart: 8 -> 7, of which waited for: 8 -> 7; matrix products, arithmetic and copies ran while one was open for 4% -> 3% of each run, Pallas kernels for 0% -> 0%
where the time goes in v1:
time: 707 us; the launch traced here: 706 us
  waiting for transfers between devices  494 us (70%)
  blocking collectives  116 us (16%)
  matrix products  39.3 us (6%)
  local copies, waits for them, and re-layouts  37.5 us (5%)
  between operations  14.8 us (2%)
    psum x2, waiting for transfers between devices, from_root(): return lax.psum(jnp.where(mine, shard, jnp.zeros_like(shard)), axis)  273 us
    all_gather x1, waiting for transfers between devices, per_device(): lax.all_gather(row_pair_slice[..., inner_feature_width:], 'gi', axis=1, t...  79 us
    all_to_all x2, blocking collectives, update_keys_all(): lax.all_to_all(jnp.stack([local for _ in range(lax.axis_size(('branch', '...  47 us
    all_gather x1, waiting for transfers between devices, per_device(): lax.all_gather(row_pair_slice[..., :inner_feature_width], 'gi', axis=1, t...  44.2 us
    all_gather x1, blocking collectives, per_device(): lax.all_gather(bias_local, ('branch', 'gj'), axis=1, tiled=True)  40.4 us
    all_gather x1, waiting for transfers between devices, panels(): lax.all_gather(second_local, ('branch', 'gj'), axis=1, tiled=True)  33.5 us
    all_gather x1, waiting for transfers between devices, per_device(): lax.all_gather(column_pairs[..., inner_feature_width:], ('branch', 'gj'),...  32.4 us
    all_gather x1, waiting for transfers between devices, per_device(): lax.all_gather(column_pairs[..., :inner_feature_width], ('branch', 'gj'),...  30.8 us
  transfers between devices with their start and end apart: 7, of which 7 were waited for; matrix products, arithmetic and copies ran while one was open for 3% of the time, Pallas kernels for 0%

profile of v1, /device:TPU:2, one launch (start us, length us, event | category | flops | bytes accessed | tf_op | source)
XLA Modules:
  0.0 706.1 jit_solution(1328618393988036790)
XLA Ops:
  9.5 1.4 fusion.100
  10.8 1.6 fusion.19
  17.4 40.4 %all_gather.22 = f32[16,2048]{0,1:T(8,128)S(1)} all-gather(f32[16,128]{0,1:T(8,128)S(1)} %convolution_bitcast_fusion.2), channel_id=1, replica_groups=mesh['branch'=2,'gi'=16,'gj'=8] {'branch','gj'}, dimensions={1}, use_global_device_ids=true | all-gather | bytes 139264 | tf_op jit(solution)/shard_map/all_gather | solution.py:101
  58.2 44.2 %all-gather.6.cloned.1.call-done = f32[8,256,256]{2,1,0:T(8,128)} async-done(((f32[8,16,256]{2,1,0:T(8,128)}), f32[8,256,256]{2,1,0:T(8,128)}) %all-gather.6.cloned.1.call-update) | async-done | bytes 2097168 | tf_op jit(solution)/shard_map/all_gather | solution.py:118
  102.4 2.9 copy.94
  105.3 2.9 fusion.101
  108.6 79.0 %all-gather.8.cloned.1.call-done = f32[8,256,256]{2,1,0:T(8,128)} async-done(((f32[8,16,256]{2,1,0:T(8,128)}), f32[8,256,256]{2,1,0:T(8,128)}) %all-gather.8.cloned.1.call-update) | async-done | bytes 2097168 | tf_op jit(solution)/shard_map/all_gather | solution.py:119
  187.7 2.9 copy.98
  190.5 3.5 fusion.1
  195.8 1.3 fusion.102
  200.6 30.8 %all-gather.10.cloned.1.call-done = f32[128,16,256]{2,1,0:T(8,128)} async-done(((f32[8,16,256]{2,1,0:T(8,128)}), f32[128,16,256]{2,1,0:T(8,128)}) %all-gather.10.cloned.1.call-update) | async-done | bytes 2097168 | tf_op jit(solution)/shard_map/all_gather | solution.py:150
  231.4 2.0 copy.100
  233.4 3.2 fusion.103
  237.7 32.4 %all-gather.12.cloned.1.call-done = f32[128,16,256]{2,1,0:T(8,128)} async-done(((f32[8,16,256]{2,1,0:T(8,128)}), f32[128,16,256]{2,1,0:T(8,128)}) %all-gather.12.cloned.1.call-update) | async-done | bytes 2097168 | tf_op jit(solution)/shard_map/all_gather | solution.py:153
  270.1 2.0 copy.102
  272.1 4.5 fusion.2
  276.9 1.6 fusion.6
  281.3 28.3 %all_gather.26 = f32[16,4096]{1,0:T(8,128)S(1)} all-gather(f32[16,256]{1,0:T(8,128)S(1)} %reshape.169), channel_id=1, replica_groups=mesh['branch'=2,'gi'=16,'gj'=8] {'branch','gj'}, dimensions={1}, use_global_device_ids=true | all-gather | bytes 278528 | tf_op jit(solution)/shard_map/all_gather | solution.py:69
  311.2 11.1 %all_to_all.10 = f32[16,16,256]{2,1,0:T(8,128)S(1)} all-to-all(f32[16,16,256]{2,1,0:T(8,128)S(1)} %stack.6), channel_id=1, replica_groups=mesh['branch'=2,'gi'=16,'gj'=8] {'branch','gj'}, dimensions={0} | all-to-all | bytes 524288 | tf_op jit(solution)/shard_map/all_to_all | solution.py:58
  322.7 145.2 %all-reduce.3.cloned.1.call-done = f32[16,128,32]{1,2,0:T(8,128)} async-done(((f32[16,128,32]{1,2,0:T(8,128)}), f32[16,128,32]{1,2,0:T(8,128)}) %all-reduce.3.cloned.1.call-update) | async-done | bytes 262160 | tf_op jit(solution)/shard_map/psum | solution.py:14
  468.0 5.9 multiply_bitcast_fusion
  473.8 5.4 copy.109
  479.2 3.8 reshape.172
  486.0 33.5 %all-gather.14.cloned.1.call-done = f32[16,32768]{1,0:T(8,128)} async-done(((f32[16,2048]{1,0:T(8,128)}), f32[16,32768]{1,0:T(8,128)}) %all-gather.14.cloned.1.call-update) | async-done | bytes 2097168 | tf_op jit(solution)/shard_map/all_gather | solution.py:69
  520.1 2.0 copy.110
  522.4 35.9 %all_to_all.11 = f32[16,16,2048]{2,1,0:T(8,128)S(1)} all-to-all(f32[16,16,2048]{2,1,0:T(8,128)S(1)} %stack.7), channel_id=1, replica_groups=mesh['branch'=2,'gi'=16,'gj'=8] {'branch','gj'}, dimensions={0} | all-to-all | bytes 4194304 | tf_op jit(solution)/shard_map/all_to_all | solution.py:58
  559.6 1.5 reshape_reshape.7
  561.1 2.2 copy.112
  563.4 127.4 %all-reduce.5.cloned.1.call-done = f32[16,256,128]{1,0,2:T(8,128)} async-done(((f32[16,256,128]{1,0,2:T(8,128)}), f32[16,256,128]{1,0,2:T(8,128)}) %all-reduce.5.cloned.1.call-update) | async-done | bytes 2097168 | tf_op jit(solution)/shard_map/psum | solution.py:14
  690.7 4.7 bitcast_reduce_fusion
  695.5 1.6 copy.113
  697.4 1.9 fusion.11
  (120 shorter events, 24.4 us)
Async XLA Ops:
  7.2 271.9 %copy-start = (f32[256,1024]{1,0:T(8,128)S(1)}, f32[256,1024]{1,0:T(8,128)}, u32[]{:S(2)}) copy-start(f32[256,1024]{1,0:T(8,128)} %param.24) | copy-start | bytes 3145732
  7.2 6.9 copy-start.3
  7.2 6.7 copy-start.5
  7.2 8.5 %copy-start.16 = (f32[3,128]{1,0:T(4,128)S(1)}, f32[3,128]{1,0:T(4,128)}, u32[]{:S(2)}) copy-start(f32[3,128]{1,0:T(4,128)} %param.18) | copy-start | bytes 4612
  7.2 9.2 %copy-start.14 = (f32[128,8]{0,1:T(8,128)S(1)}, f32[128,8]{0,1:T(8,128)}, u32[]{:S(2)}) copy-start(f32[128,8]{0,1:T(8,128)} %param.19) | copy-start | bytes 12292
  7.2 95.1 %all-gather.6.cloned.1.call-start = ((), (), s32[]{:S(2)}) async-start(), calls=%async_computation.2 | async-start | bytes 2228224 | tf_op jit(solution)/shard_map/all_gather | solution.py:118
  13.1 174.5 %all-gather.8.cloned.1.call-start = ((), (), s32[]{:S(2)}) async-start(), calls=%async_computation.3 | async-start | bytes 2228224 | tf_op jit(solution)/shard_map/all_gather | solution.py:119
  13.9 217.5 %all-gather.10.cloned.1.call-start = ((), (), s32[]{:S(2)}) async-start(), calls=%async_computation.4 | async-start | bytes 2228224 | tf_op jit(solution)/shard_map/all_gather | solution.py:150
  194.1 3.2 copy-start.8
  198.5 71.6 %all-gather.12.cloned.1.call-start = ((), (), s32[]{:S(2)}) async-start(), calls=%async_computation.5 | async-start | bytes 2228224 | tf_op jit(solution)/shard_map/all_gather | solution.py:153
  199.1 268.9 %all-reduce.3.cloned.1.call-start = ((), (), s32[]{:S(2)}) async-start(), calls=%async_computation.6 | async-start | bytes 524288 | tf_op jit(solution)/shard_map/psum | solution.py:14
  236.5 0.8 copy-start.2
  276.5 1.9 copy-start.11
  276.6 2.5 copy-start.13
  276.7 3.2 copy-start.7
  278.9 1.9 copy-start.12
  280.5 30.5 %copy-start.6 = (f32[8,16,256]{2,1,0:T(8,128)}, f32[8,16,256]{2,1,0:T(8,128)S(1)}, u32[]{:S(2)}) copy-start(f32[8,16,256]{2,1,0:T(8,128)S(1)} %get-tuple-element.26) | copy-start | bytes 393220
  311.0 208.5 %all-gather.14.cloned.1.call-start = ((), (), s32[]{:S(2)}) async-start(), calls=%async_computation.7 | async-start | bytes 2228224 | tf_op jit(solution)/shard_map/all_gather | solution.py:69
  479.2 3.8 copy-start.9
  479.2 5.1 copy-start.15
  483.0 1.3 copy-start.10
  485.1 34.6 %copy-start.4 = (f32[16,16,640]{2,1,0:T(8,128)}, f32[16,16,640]{2,1,0:T(8,128)S(1)}, u32[]{:S(2)}) copy-start(f32[16,16,640]{2,1,0:T(8,128)S(1)} %fusion.27) | copy-start | bytes 1966084
  486.0 204.7 %all-reduce.5.cloned.1.call-start = ((), (), s32[]{:S(2)}) async-start(), calls=%async_computation.8 | async-start | bytes 4194304 | tf_op jit(solution)/shard_map/psum | solution.py:14
  563.3 134.0 %copy-start.17 = (f32[128]{0:T(128)S(1)}, f32[128]{0:T(128)}, u32[]{:S(2)}) copy-start(f32[128]{0:T(128)} %get-tuple-element.14) | copy-start | bytes 1540
  563.4 134.0 %copy-start.18 = (f32[128,128]{1,0:T(8,128)S(1)}, f32[128,128]{1,0:T(8,128)}, u32[]{:S(2)}) copy-start(f32[128,128]{1,0:T(8,128)} %param.29) | copy-start | bytes 196612
  690.7 8.6 %copy-start.1 = (f32[256,1024]{1,0:T(8,128)S(1)}, f32[256,1024]{1,0:T(8,128)}, u32[]{:S(2)}) copy-start(f32[256,1024]{1,0:T(8,128)} %param.24) | copy-start | bytes 3145732
Sparse Core Ops, SparseCore 0:
  13.3 89.0 all-gather.5
  105.5 82.0 all-gather.7
  198.6 32.7 all-gather.9
  233.6 36.3 all-gather.11
  311.2 156.7 all-reduce.2
  486.1 33.3 all-gather.13
  522.3 168.3 all-reduce.4
